TPU v7x, 32 devices: a whole 2x2x4 slice. The times are simulated.
32 devices in a mesh: row: 8 (over y, x, core), col: 4 (over z).
Axes of the slice: x: 2, y: 2, z: 4, core: 2. Of those that a mesh axis runs over, the one named last changes fastest.
Arguments:
- features: bfloat16 [16384, 512], P(('row', 'col')), may hold values from -6 to 6
- weight: bfloat16 [512, 512], replicated, may hold values from -0.25 to 0.25
- bias: float32 [512], replicated, may hold values from -3 to 3
- cotangent: bfloat16 [16384, 512], P(('row', 'col')), may hold values from -6 to 6
- tile_values: bfloat16 [8, 4, 64, 128, 128], P('row', 'col'), may hold values from -0.1875 to 0.1875
- tile_rows: int32 [8, 4, 64], P('row', 'col'), may hold values from 0 to 127, as said below
- tile_cols: int32 [8, 4, 64], P('row', 'col'), may hold values from 0 to 127, as said below
- tile_counts: int32 [8, 4], P('row', 'col'), may hold values from 1 to 64
Outputs:
- output: bfloat16 [16384, 512], P(('row', 'col'))
- feature_grad: bfloat16 [16384, 512], P(('row', 'col'))
- weight_grad: float32 [512, 512], replicated
- bias_grad: float32 [512], replicated
Inputs may be any that keep to these rules, and one draw needn't show every extreme that they name: `tile_rows`: A tile on device (p, q) has its row block in row group p, that is row block // 16 == p, and its column block's atoms on devices of index q along col, that is (column block // 4) % 4 == q. The rows of features held by device (p, q) are blocks p * 4 * 4 + q * 4 to that plus 4 - 1. Row and column pairs may repeat. `tile_cols`: among one device's live tiles at most 16 have their row block held by any one device of that row group, and at most 8 have their column block held by any one device of that column group.
All inputs are finite; a program needn't handle non-finite values.
Results may differ from a plain program's by a relative error of at most 0.013.
Values may be sent and summed in bfloat16 or wider, within the bound.
A program may use at most 128 MiB of HBM per device.

v0:
```python
import math
import jax
import jax.numpy as jnp
from jax import lax
from jax.sharding import PartitionSpec as P


def sum_rows(products, local_ids, alive_mask, total_blocks):
    block_size = products.shape[1]
    feature_width = products.shape[2]
    target_ids = jnp.where(alive_mask, local_ids, total_blocks)
    blank_sum = jnp.zeros((total_blocks, block_size, feature_width), jnp.float32)
    summed = blank_sum.at[target_ids].add(products, mode="drop")
    return summed.reshape(total_blocks * block_size, feature_width)


def on_device(features, weight, bias, cotangent, tile_values, tile_rows, tile_cols, tile_counts):
    row_count = lax.axis_size("row")
    col_count = lax.axis_size("col")
    node_dev, feature_width = features.shape
    slot_count = tile_values.shape[2]
    block_size = tile_values.shape[3]
    blk_dev = node_dev // block_size
    atom_count = node_dev * row_count * col_count
    values = tile_values.reshape(slot_count, block_size, block_size)
    alive_mask = jnp.arange(slot_count) < tile_counts.reshape(())
    row_local = tile_rows.reshape(slot_count) % (blk_dev * col_count)
    col_ids = tile_cols.reshape(slot_count)
    col_local = col_ids // (blk_dev * col_count) * blk_dev + col_ids % blk_dev
    gathered = lax.all_gather(features, "row", axis=0, tiled=True).reshape(
        row_count * blk_dev, block_size, feature_width
    )
    sources = gathered[col_local]
    products = jnp.einsum("kab,kbd->kad", values, sources, preferred_element_type=jnp.float32)
    partial_value = sum_rows(products, row_local, alive_mask, blk_dev * col_count)
    summed = lax.psum_scatter(partial_value, "col", scatter_dimension=0, tiled=True)
    aggregated = summed.astype(jnp.bfloat16)
    pre_act = jnp.dot(aggregated, weight, preferred_element_type=jnp.float32) + bias
    sigm = jax.nn.sigmoid(pre_act)
    output = (pre_act * sigm).astype(jnp.bfloat16)
    grad_pre = (cotangent.astype(jnp.float32) * sigm * (1.0 + pre_act * (1.0 - sigm))).astype(
        jnp.bfloat16
    )
    scale = 1.0 / math.sqrt(atom_count)
    weight_part = jnp.dot(aggregated.T, grad_pre, preferred_element_type=jnp.float32) * scale
    bias_part = jnp.sum(grad_pre.astype(jnp.float32), axis=0) * scale
    weight_grad, bias_grad = lax.psum((weight_part, bias_part), ("row", "col"))
    grad_agg = jnp.dot(grad_pre, weight.T, preferred_element_type=jnp.float32).astype(jnp.bfloat16)
    spread = lax.all_gather(grad_agg, "col", axis=0, tiled=True).reshape(
        col_count * blk_dev, block_size, feature_width
    )
    upstream = spread[row_local]
    back_products = jnp.einsum("kba,kbd->kad", values, upstream, preferred_element_type=jnp.float32)
    grad_partial = sum_rows(back_products, col_local, alive_mask, blk_dev * row_count)
    grad_summed = lax.psum_scatter(
        grad_partial.astype(jnp.bfloat16), "row", scatter_dimension=0, tiled=True
    )
    return (output, grad_summed, weight_grad, bias_grad)


def solution(mesh):
    return jax.shard_map(
        on_device,
        mesh=mesh,
        in_specs=(
            P(("row", "col"), None),
            P(),
            P(),
            P(("row", "col"), None),
            P("row", "col", None, None, None),
            P("row", "col", None),
            P("row", "col", None),
            P("row", "col"),
        ),
        out_specs=(P(("row", "col"), None), P(("row", "col"), None), P(), P()),
        check_vma=False,
    )
```

profile of v0, /device:TPU:0, one launch (start us, length us, event | category | flops | bytes accessed | tf_op | source)
XLA Modules:
  0.0 449.0 jit_solution(17194235437523508426)
XLA Ops:
  7.2 0.7 all-gather.3.cloned.1.call-update
  8.6 0.7 fusion.8
  9.3 0.7 fusion.9
  10.0 39.2 %all-gather.3.cloned.1.call-done = bf16[4096,512]{1,0:T(8,128)(2,1)} async-done(((bf16[512,512]{1,0:T(8,128)(2,1)}), bf16[4096,512]{1,0:T(8,128)(2,1)}) %all-gather.3.cloned.1.call-update) | async-done | bytes 4194320 | tf_op jit(solution)/shard_map/all_gather | solution.py:30
  49.2 7.7 %gather_fusion = bf16[64,128,512]{2,1,0:T(8,128)(2,1)} fusion(bf16[32,128,512]{2,1,0:T(8,128)(2,1)} %bitcast.47, s32[1024]{0:T(1024)S(1)} %pad_clamp_fusion.1), kind=kCustom, calls=%fused_computation | custom fusion | bytes 16777472 | tf_op jit(solution)/shard_map/gather | solution.py:33
  56.9 11.5 %convolution_bitcast_fusion.1 = f32[64,128,512]{1,2,0:T(8,128)} fusion(bf16[64,128,512]{2,1,0:T(8,128)(2,1)} %gather_fusion, bf16[1,1,64,128,128]{4,3,2,1,0:T(8,128)(2,1)S(1)} %copy-done), kind=kOutput, calls=%fused_computation.5 | convolution fusion | flops 1073741824 | bytes 27262976 | tf_op jit(solution)/shard_map/kab,kbd->kad/dot_general | solution.py:34
  68.4 17.5 %copy.15 = f32[64,128,512]{2,1,0:T(8,128)} copy(f32[64,128,512]{1,2,0:T(8,128)} %convolution_bitcast_fusion.1) | data formatting | bytes 33554432 | tf_op jit(solution)/shard_map/kab,kbd->kad/dot_general | solution.py:34
  85.9 2.5 broadcast_in_dim.7
  88.4 34.5 %scatter_fusion = f32[16,128,512]{2,1,0:T(8,128)} fusion(f32[16,128,512]{2,1,0:T(8,128)} %broadcast_in_dim.7, s32[64]{0:T(128)S(1)} %fusion.6, f32[64,128,512]{2,1,0:T(8,128)} %copy.15), kind=kCustom, calls=%fused_computation.2 | custom fusion | flops 4194304 | bytes 50331904 | tf_op jit(solution)/shard_map/scatter-add | solution.py:13
  122.9 77.6 %reduce-scatter.3.cloned.1.call-done = f32[512,512]{1,0:T(8,128)} async-done(((f32[2048,512]{1,0:T(8,128)}), f32[512,512]{1,0:T(8,128)}) %reduce-scatter.3.cloned.1.call-update) | async-done | bytes 1048592 | tf_op jit(solution)/shard_map/reduce_scatter | solution.py:36
  200.5 3.0 convert_reduce_fusion
  203.5 1.3 convolution_convert_fusion
  204.9 2.7 convolution_multiply_fusion
  207.8 43.3 %all-gather.5.cloned.1.call-done = bf16[2048,512]{1,0:T(8,128)(2,1)} async-done(((bf16[512,512]{1,0:T(8,128)(2,1)}), bf16[2048,512]{1,0:T(8,128)(2,1)}) %all-gather.5.cloned.1.call-update) | async-done | bytes 2097168 | tf_op jit(solution)/shard_map/all_gather | solution.py:49
  251.1 7.1 %gather_fusion.1 = bf16[64,128,512]{2,1,0:T(8,128)(2,1)} fusion(bf16[16,128,512]{2,1,0:T(8,128)(2,1)} %bitcast.46, s32[1024]{0:T(1024)S(1)} %pad_clamp_fusion), kind=kCustom, calls=%fused_computation.1 | custom fusion | bytes 16777472 | tf_op jit(solution)/shard_map/gather | solution.py:52
  258.2 11.6 %convolution_bitcast_fusion = f32[64,128,512]{1,2,0:T(8,128)} fusion(bf16[64,128,512]{2,1,0:T(8,128)(2,1)} %gather_fusion.1, bf16[1,1,64,128,128]{4,3,2,1,0:T(8,128)(2,1)S(1)} %copy-done), kind=kOutput, calls=%fused_computation.4 | convolution fusion | flops 1073741824 | bytes 27262976 | tf_op jit(solution)/shard_map/kba,kbd->kad/dot_general | solution.py:53
  269.8 17.5 %copy.17 = f32[64,128,512]{2,1,0:T(8,128)} copy(f32[64,128,512]{1,2,0:T(8,128)} %convolution_bitcast_fusion) | data formatting | bytes 33554432 | tf_op jit(solution)/shard_map/kba,kbd->kad/dot_general | solution.py:53
  287.3 4.3 broadcast_in_dim.8
  291.6 34.7 %scatter_fusion.1 = f32[32,128,512]{2,1,0:T(8,128)} fusion(f32[32,128,512]{2,1,0:T(8,128)} %broadcast_in_dim.8, s32[64]{0:T(128)S(1)} %get-tuple-element.8, f32[64,128,512]{2,1,0:T(8,128)} %copy.17), kind=kCustom, calls=%fused_computation.3 | custom fusion | flops 4194304 | bytes 50331904 | tf_op jit(solution)/shard_map/scatter-add | solution.py:13
  326.3 5.9 %convert_element_type.29 = bf16[32,128,512]{2,1,0:T(8,128)(2,1)} convert(f32[32,128,512]{2,1,0:T(8,128)} %scatter_fusion.1) | non-fusion elementwise | flops 2097152 | bytes 12582912 | tf_op jit(solution)/shard_map/convert_element_type | solution.py:56
  332.3 39.5 %psum.15 = f32[512]{0:T(512)} all-reduce(f32[512]{0:T(512)S(1)} %broadcast_multiply_fusion), channel_id=1, replica_groups=mesh['row'=8,'col'=4] {'row','col'}, use_global_device_ids=true, to_apply=%region_6.7 | all-reduce | flops 512 | bytes 4096 | tf_op jit(solution)/shard_map/psum | solution.py:47
  371.8 14.5 %all-reduce.2.cloned.1.call-done = f32[512,512]{1,0:T(8,128)} async-done(((f32[512,512]{1,0:T(8,128)}), f32[512,512]{1,0:T(8,128)}) %all-reduce.2.cloned.1.call-update) | async-done | bytes 1048592 | tf_op jit(solution)/shard_map/psum | solution.py:47
  386.3 53.9 %reduce-scatter.5.cloned.1.call-done = bf16[512,512]{1,0:T(8,128)(2,1)} async-done(((bf16[4096,512]{1,0:T(8,128)(2,1)}), bf16[512,512]{1,0:T(8,128)(2,1)}) %reduce-scatter.5.cloned.1.call-update) | async-done | bytes 524304 | tf_op jit(solution)/shard_map/reduce_scatter | solution.py:55
  440.2 2.3 copy.24
  (20 shorter events, 0.5 us)
Async XLA Ops:
  7.2 49.8 %copy-start = (bf16[1,1,64,128,128]{4,3,2,1,0:T(8,128)(2,1)S(1)}, bf16[1,1,64,128,128]{4,3,2,1,0:T(8,128)(2,1)}, u32[]{:S(2)}) copy-start(bf16[1,1,64,128,128]{4,3,2,1,0:T(8,128)(2,1)} %param.12) | copy-start | bytes 6291460
  7.2 42.0 %all-gather.3.cloned.1.call-start = ((), (), s32[]{:S(2)}) async-start(), calls=%async_computation.2 | async-start | bytes 4718592 | tf_op jit(solution)/shard_map/all_gather | solution.py:30
  7.9 192.6 %reduce-scatter.3.cloned.1.call-start = ((), (), s32[]{:S(2)}) async-start(), calls=%async_computation.3 | async-start | bytes 5242880 | tf_op jit(solution)/shard_map/reduce_scatter | solution.py:36
  88.4 112.2 %copy-start.1 = (bf16[512,512]{1,0:T(8,128)(2,1)S(1)}, bf16[512,512]{1,0:T(8,128)(2,1)}, u32[]{:S(2)}) copy-start(bf16[512,512]{1,0:T(8,128)(2,1)} %param.9) | copy-start | bytes 1572868
  88.4 112.2 %copy-start.2 = (f32[512]{0:T(512)S(1)}, f32[512]{0:T(512)}, u32[]{:S(2)}) copy-start(f32[512]{0:T(512)} %param.10) | copy-start | bytes 6148
  122.8 128.3 %all-gather.5.cloned.1.call-start = ((), (), s32[]{:S(2)}) async-start(), calls=%async_computation.4 | async-start | bytes 2621440 | tf_op jit(solution)/shard_map/all_gather | solution.py:49
  204.8 181.5 %all-reduce.2.cloned.1.call-start = ((), (), s32[]{:S(2)}) async-start(), calls=%async_computation.6 | async-start | bytes 2097152 | tf_op jit(solution)/shard_map/psum | solution.py:47
  207.6 232.7 %reduce-scatter.5.cloned.1.call-start = ((), (), s32[]{:S(2)}) async-start(), calls=%async_computation.5 | async-start | bytes 4718592 | tf_op jit(solution)/shard_map/reduce_scatter | solution.py:55
Sparse Core Ops, SparseCore 0:
  9.9 39.2 all-gather.2
  123.0 77.4 reduce-scatter.2
  204.9 46.1 all-gather.4
  256.7 129.5 all-reduce.1
  390.1 50.0 reduce-scatter.4
where the time goes:
time: 450 us; the launch traced here: 449 us
  waiting for transfers between devices  229 us (51%)
  other arithmetic  76.5 us (17%)
  local copies, waits for them, and re-layouts  58.8 us (13%)
  blocking collectives  39.5 us (9%)
  matrix products  30 us (7%)
  between operations  14.5 us (3%)
    reduce_scatter x1, waiting for transfers between devices, on_device(): lax.psum_scatter(partial_value, 'col', scatter_dimension=0, tiled=True)  77.6 us
    scatter-add x2, other arithmetic, sum_rows(): summed = blank_sum.at[target_ids].add(products, mode='drop')  69.2 us
    reduce_scatter x1, waiting for transfers between devices, on_device(): lax.psum_scatter(grad_partial.astype(jnp.bfloat16), 'row', scatter_dimens...  53.9 us
    all_gather x1, waiting for transfers between devices, on_device(): lax.all_gather(grad_agg, 'col', axis=0, tiled=True)  43.3 us
    psum x1, blocking collectives, on_device(): weight_grad, bias_grad = lax.psum((weight_part, bias_part), ('row', 'col'))  39.5 us
    all_gather x1, waiting for transfers between devices, on_device(): lax.all_gather(features, 'row', axis=0, tiled=True)  39.2 us
    dot_general x1, local copies, waits for them, and re-layouts, on_device(): jnp.einsum('kba,kbd->kad', values, upstream, preferred_element_type=jnp.f...  17.5 us
    dot_general x1, local copies, waits for them, and re-layouts, on_device(): jnp.einsum('kab,kbd->kad', values, sources, preferred_element_type=jnp.fl...  17.5 us
  transfers between devices with their start and end apart: 5, of which 5 were waited for; matrix products, arithmetic and copies ran while one was open for 19% of the time, Pallas kernels for 0%

commit v1 on v0

--- a/solution.py
+++ b/solution.py
@@ -3,6 +3,23 @@
 import jax.numpy as jnp
 from jax import lax
 from jax.sharding import PartitionSpec as P
+
+
+def in_order(blocks, dim):
+    shape = list(blocks.shape[1:])
+    shape[dim] *= blocks.shape[0]
+    return jnp.moveaxis(blocks, 0, dim).reshape(shape)
+
+
+def ring_gather(x, axis, dim):
+    size = lax.axis_size(axis)
+    right = [(i, (i + 1) % size) for i in range(size)]
+    parts = [x]
+    while len(parts) < size:
+        parts.append(lax.ppermute(parts[-1], axis, right))
+    index = lax.axis_index(axis)
+    parts = jnp.stack(parts)[(index - jnp.arange(size)) % size]
+    return in_order(parts, dim)
 
 
 def sum_rows(products, local_ids, alive_mask, total_blocks):
@@ -46,9 +63,7 @@
     bias_part = jnp.sum(grad_pre.astype(jnp.float32), axis=0) * scale
     weight_grad, bias_grad = lax.psum((weight_part, bias_part), ("row", "col"))
     grad_agg = jnp.dot(grad_pre, weight.T, preferred_element_type=jnp.float32).astype(jnp.bfloat16)
-    spread = lax.all_gather(grad_agg, "col", axis=0, tiled=True).reshape(
-        col_count * blk_dev, block_size, feature_width
-    )
+    spread = ring_gather(grad_agg, "col", 0).reshape(col_count * blk_dev, block_size, feature_width)
     upstream = spread[row_local]
     back_products = jnp.einsum("kba,kbd->kad", values, upstream, preferred_element_type=jnp.float32)
     grad_partial = sum_rows(back_products, col_local, alive_mask, blk_dev * row_count)

time: 450 us -> 434 us (0.964)
  waiting for transfers between devices: 229 us -> 208 us
    all_gather x1 -> x0, waiting for transfers between devices: 43.3 us -> none  [on_device(): lax.all_gather(grad_agg, 'col', axis=0, tiled=True)]
    ppermute x0 -> x3, waiting for transfers between devices: none -> 39.3 us  [ring_gather(): parts.append(lax.ppermute(parts[-1], axis, right))]
    psum x1, waiting for transfers between devices: 14.5 us -> 0.01 us  [on_device(): weight_grad, bias_grad = lax.psum((weight_part, bias_part), ('row', 'col'))]
  transfers between devices with their start and end apart: 5 -> 7, of which waited for: 5 -> 6; matrix products, arithmetic and copies ran while one was open for 19% -> 21% of each run, Pallas kernels for 0% -> 0%
where the time goes in v1:
time: 434 us; the launch traced here: 433 us
  waiting for transfers between devices  208 us (48%)
  other arithmetic  79.4 us (18%)
  local copies, waits for them, and re-layouts  62.5 us (14%)
  blocking collectives  37.1 us (9%)
  matrix products  30.2 us (7%)
  between operations  14.5 us (3%)
    reduce_scatter x1, waiting for transfers between devices, on_device(): lax.psum_scatter(partial_value, 'col', scatter_dimension=0, tiled=True)  77.6 us
    scatter-add x2, other arithmetic, sum_rows(): summed = blank_sum.at[target_ids].add(products, mode='drop')  69.1 us
    reduce_scatter x1, waiting for transfers between devices, on_device(): lax.psum_scatter(grad_partial.astype(jnp.bfloat16), 'row', scatter_dimens...  50.9 us
    ppermute x3, waiting for transfers between devices, ring_gather(): parts.append(lax.ppermute(parts[-1], axis, right))  39.3 us
    all_gather x1, waiting for transfers between devices, on_device(): lax.all_gather(features, 'row', axis=0, tiled=True)  39.2 us
    psum x1, blocking collectives, on_device(): weight_grad, bias_grad = lax.psum((weight_part, bias_part), ('row', 'col'))  37.1 us
    dot_general x1, local copies, waits for them, and re-layouts, on_device(): jnp.einsum('kba,kbd->kad', values, upstream, preferred_element_type=jnp.f...  17.5 us
    dot_general x1, local copies, waits for them, and re-layouts, on_device(): jnp.einsum('kab,kbd->kad', values, sources, preferred_element_type=jnp.fl...  17.5 us
  transfers between devices with their start and end apart: 7, of which 6 were waited for; matrix products, arithmetic and copies ran while one was open for 21% of the time, Pallas kernels for 0%

profile of v1, /device:TPU:0, one launch (start us, length us, event | category | flops | bytes accessed | tf_op | source)
XLA Modules:
  0.0 433.3 jit_solution(2334395772752603628)
XLA Ops:
  10.0 39.2 %all-gather.2.cloned.1.call-done = bf16[4096,512]{1,0:T(8,128)(2,1)} async-done(((bf16[512,512]{1,0:T(8,128)(2,1)}), bf16[4096,512]{1,0:T(8,128)(2,1)}) %all-gather.2.cloned.1.call-update) | async-done | bytes 4194320 | tf_op jit(solution)/shard_map/all_gather | solution.py:47
  49.2 7.7 %gather_fusion = bf16[64,128,512]{2,1,0:T(8,128)(2,1)} fusion(bf16[32,128,512]{2,1,0:T(8,128)(2,1)} %bitcast.53, s32[1024]{0:T(1024)S(1)} %pad_clamp_fusion.2), kind=kCustom, calls=%fused_computation | custom fusion | bytes 16777472 | tf_op jit(solution)/shard_map/gather | solution.py:50
  56.9 11.5 %convolution_bitcast_fusion.1 = f32[64,128,512]{1,2,0:T(8,128)} fusion(bf16[64,128,512]{2,1,0:T(8,128)(2,1)} %gather_fusion, bf16[1,1,64,128,128]{4,3,2,1,0:T(8,128)(2,1)S(1)} %copy-done), kind=kOutput, calls=%fused_computation.6 | convolution fusion | flops 1073741824 | bytes 27262976 | tf_op jit(solution)/shard_map/kab,kbd->kad/dot_general | solution.py:51
  68.4 17.5 %copy.15 = f32[64,128,512]{2,1,0:T(8,128)} copy(f32[64,128,512]{1,2,0:T(8,128)} %convolution_bitcast_fusion.1) | data formatting | bytes 33554432 | tf_op jit(solution)/shard_map/kab,kbd->kad/dot_general | solution.py:51
  85.9 2.5 broadcast_in_dim.7
  88.4 34.5 %scatter_fusion = f32[16,128,512]{2,1,0:T(8,128)} fusion(f32[16,128,512]{2,1,0:T(8,128)} %broadcast_in_dim.7, s32[64]{0:T(128)S(1)} %fusion.7, f32[64,128,512]{2,1,0:T(8,128)} %copy.15), kind=kCustom, calls=%fused_computation.3 | custom fusion | flops 4194304 | bytes 50331904 | tf_op jit(solution)/shard_map/scatter-add | solution.py:30
  122.9 77.6 %reduce-scatter.3.cloned.1.call-done = f32[512,512]{1,0:T(8,128)} async-done(((f32[2048,512]{1,0:T(8,128)}), f32[512,512]{1,0:T(8,128)}) %reduce-scatter.3.cloned.1.call-update) | async-done | bytes 1048592 | tf_op jit(solution)/shard_map/reduce_scatter | solution.py:53
  200.5 3.0 convert_reduce_fusion
  205.0 1.5 collective-permute-start
  206.6 13.8 %collective-permute-done = bf16[512,512]{1,0:T(8,128)(2,1)} collective-permute-done((bf16[512,512]{1,0:T(8,128)(2,1)S(1)}, bf16[512,512]{1,0:T(8,128)(2,1)}, u32[]{:S(2)}, u32[]{:S(2)}) %collective-permute-start) | collective-permute-done | bytes 524320 | tf_op jit(solution)/shard_map/ppermute | solution.py:19
  220.3 14.6 %collective-permute-done.1 = bf16[512,512]{1,0:T(8,128)(2,1)} collective-permute-done((bf16[512,512]{1,0:T(8,128)(2,1)}, bf16[512,512]{1,0:T(8,128)(2,1)}, u32[]{:S(2)}, u32[]{:S(2)}) %collective-permute-start.1) | collective-permute-done | bytes 524320 | tf_op jit(solution)/shard_map/ppermute | solution.py:19
  235.0 2.7 convolution_multiply_fusion
  237.9 10.9 %collective-permute-done.2 = bf16[512,512]{1,0:T(8,128)(2,1)} collective-permute-done((bf16[512,512]{1,0:T(8,128)(2,1)}, bf16[512,512]{1,0:T(8,128)(2,1)}, u32[]{:S(2)}, u32[]{:S(2)}) %collective-permute-start.2) | collective-permute-done | bytes 524320 | tf_op jit(solution)/shard_map/ppermute | solution.py:19
  248.8 3.0 pad_maximum_fusion
  251.8 3.7 gather_fusion.1
  255.4 7.1 %gather_fusion.2 = bf16[64,128,512]{2,1,0:T(8,128)(2,1)} fusion(bf16[16,128,512]{2,1,0:T(8,128)(2,1)} %bitcast.52, s32[1024]{0:T(1024)S(1)} %pad_clamp_fusion), kind=kCustom, calls=%fused_computation.2 | custom fusion | bytes 16777472 | tf_op jit(solution)/shard_map/gather | solution.py:67
  262.6 11.5 %convolution_bitcast_fusion = f32[64,128,512]{1,2,0:T(8,128)} fusion(bf16[64,128,512]{2,1,0:T(8,128)(2,1)} %gather_fusion.2, bf16[1,1,64,128,128]{4,3,2,1,0:T(8,128)(2,1)S(1)} %copy-done), kind=kOutput, calls=%fused_computation.5 | convolution fusion | flops 1073741824 | bytes 27262976 | tf_op jit(solution)/shard_map/kba,kbd->kad/dot_general | solution.py:68
  274.1 17.5 %copy.17 = f32[64,128,512]{2,1,0:T(8,128)} copy(f32[64,128,512]{1,2,0:T(8,128)} %convolution_bitcast_fusion) | data formatting | bytes 33554432 | tf_op jit(solution)/shard_map/kba,kbd->kad/dot_general | solution.py:68
  291.6 4.3 broadcast_in_dim.8
  295.9 34.6 %scatter_fusion.1 = f32[32,128,512]{2,1,0:T(8,128)} fusion(f32[32,128,512]{2,1,0:T(8,128)} %broadcast_in_dim.8, s32[64]{0:T(128)S(1)} %get-tuple-element.8, f32[64,128,512]{2,1,0:T(8,128)} %copy.17), kind=kCustom, calls=%fused_computation.4 | custom fusion | flops 4194304 | bytes 50331904 | tf_op jit(solution)/shard_map/scatter-add | solution.py:30
  330.5 6.0 %convert_element_type.29 = bf16[32,128,512]{2,1,0:T(8,128)(2,1)} convert(f32[32,128,512]{2,1,0:T(8,128)} %scatter_fusion.1) | non-fusion elementwise | flops 2097152 | bytes 12582912 | tf_op jit(solution)/shard_map/convert_element_type | solution.py:71
  336.5 37.1 %psum.15 = f32[512]{0:T(512)} all-reduce(f32[512]{0:T(512)S(1)} %broadcast_multiply_fusion), channel_id=1, replica_groups=mesh['row'=8,'col'=4] {'row','col'}, use_global_device_ids=true, to_apply=%region_6.7 | all-reduce | flops 512 | bytes 4096 | tf_op jit(solution)/shard_map/psum | solution.py:64
  373.6 50.9 %reduce-scatter.5.cloned.1.call-done = bf16[512,512]{1,0:T(8,128)(2,1)} async-done(((bf16[4096,512]{1,0:T(8,128)(2,1)}), bf16[512,512]{1,0:T(8,128)(2,1)}) %reduce-scatter.5.cloned.1.call-update) | async-done | bytes 524304 | tf_op jit(solution)/shard_map/reduce_scatter | solution.py:70
  424.5 2.3 copy.24
  (27 shorter events, 4.0 us)
Async XLA Ops:
  7.2 49.8 %copy-start = (bf16[1,1,64,128,128]{4,3,2,1,0:T(8,128)(2,1)S(1)}, bf16[1,1,64,128,128]{4,3,2,1,0:T(8,128)(2,1)}, u32[]{:S(2)}) copy-start(bf16[1,1,64,128,128]{4,3,2,1,0:T(8,128)(2,1)} %param.12) | copy-start | bytes 6291460
  7.2 42.0 %all-gather.2.cloned.1.call-start = ((), (), s32[]{:S(2)}) async-start(), calls=%async_computation.2 | async-start | bytes 4718592 | tf_op jit(solution)/shard_map/all_gather | solution.py:47
  7.9 192.6 %reduce-scatter.3.cloned.1.call-start = ((), (), s32[]{:S(2)}) async-start(), calls=%async_computation.3 | async-start | bytes 5242880 | tf_op jit(solution)/shard_map/reduce_scatter | solution.py:53
  88.4 112.2 %copy-start.1 = (bf16[512,512]{1,0:T(8,128)(2,1)S(1)}, bf16[512,512]{1,0:T(8,128)(2,1)}, u32[]{:S(2)}) copy-start(bf16[512,512]{1,0:T(8,128)(2,1)} %param.9) | copy-start | bytes 1572868
  88.4 112.2 %copy-start.2 = (f32[512]{0:T(512)S(1)}, f32[512]{0:T(512)}, u32[]{:S(2)}) copy-start(f32[512]{0:T(512)} %param.10) | copy-start | bytes 6148
  122.8 250.8 %all-reduce.2.cloned.1.call-start = ((), (), s32[]{:S(2)}) async-start(), calls=%async_computation.5 | async-start | bytes 2097152 | tf_op jit(solution)/shard_map/psum | solution.py:64
  205.0 15.3 %collective-permute-start = (bf16[512,512]{1,0:T(8,128)(2,1)S(1)}, bf16[512,512]{1,0:T(8,128)(2,1)}, u32[]{:S(2)}, u32[]{:S(2)}) collective-permute-start(bf16[512,512]{1,0:T(8,128)(2,1)S(1)} %convolution_convert_fusion), channel_id=1, source_target_pairs={{0,1},{1,2},{2,3},{3,0},{4,5},{5,6},{6,7},{7,4},{8,9},{9,10},{10,1... | collective-permute-start | bytes 1572872 | tf_op jit(solution)/shard_map/ppermute | solution.py:19
  220.3 14.6 %collective-permute-start.1 = (bf16[512,512]{1,0:T(8,128)(2,1)}, bf16[512,512]{1,0:T(8,128)(2,1)}, u32[]{:S(2)}, u32[]{:S(2)}) collective-permute-start(bf16[512,512]{1,0:T(8,128)(2,1)} %collective-permute-done), channel_id=1, source_target_pairs={{0,1},{1,2},{2,3},{3,0},{4,5},{5,6},{6,7},{7,4},{8,9},{9,10},{10,1... | collective-permute-start | bytes 1572872 | tf_op jit(solution)/shard_map/ppermute | solution.py:19
  235.0 13.9 %collective-permute-start.2 = (bf16[512,512]{1,0:T(8,128)(2,1)}, bf16[512,512]{1,0:T(8,128)(2,1)}, u32[]{:S(2)}, u32[]{:S(2)}) collective-permute-start(bf16[512,512]{1,0:T(8,128)(2,1)} %collective-permute-done.1), channel_id=1, source_target_pairs={{0,1},{1,2},{2,3},{3,0},{4,5},{5,6},{6,7},{7,4},{8,9},{9,10},{10,1... | collective-permute-start | bytes 1572872 | tf_op jit(solution)/shard_map/ppermute | solution.py:19
  237.7 186.8 %reduce-scatter.5.cloned.1.call-start = ((), (), s32[]{:S(2)}) async-start(), calls=%async_computation.4 | async-start | bytes 4718592 | tf_op jit(solution)/shard_map/reduce_scatter | solution.py:70
Sparse Core Ops, SparseCore 0:
  9.9 39.2 all-gather.1
  123.0 77.4 reduce-scatter.2
  237.8 132.7 all-reduce.1
  374.4 50.1 reduce-scatter.4
